TPU v7x, 256 devices: a whole 4x4x8 slice. The times are simulated.
256 devices in a mesh: hid: 32 (over x, z), tok: 8 (over y, core).
Axes of the slice: x: 4, y: 4, z: 8, core: 2. Of those that a mesh axis runs over, the one named last changes fastest.
Arguments:
- tokens: bfloat16 [2048, 12288], P('tok', 'hid'), may hold values from -6 to 6
- cotangent: bfloat16 [2048, 12288], P('tok', 'hid'), may hold values from -0.75 to 0.75
- up_tiles: bfloat16 [6, 256, 24576], P(None, None, 'hid'), may hold values from -0.15625 to 0.15625
- down_tiles: bfloat16 [6, 24576, 256], P(None, 'hid'), may hold values from -0.109375 to 0.109375
- block_index: int32 [6, 96, 2], P(None, 'hid'), may hold values from 0 to 2, as said below
- up_left: bfloat16 [12288, 256], P('hid'), may hold values from -0.0546875 to 0.0546875
- up_right: bfloat16 [256, 24576], P(None, 'hid'), may hold values from -0.375 to 0.375
- down_left: bfloat16 [24576, 256], P('hid'), may hold values from -0.0390625 to 0.0390625
- down_right: bfloat16 [256, 12288], P(None, 'hid'), may hold values from -0.375 to 0.375
Outputs:
- layer_out: bfloat16 [2048, 12288], P('tok', 'hid')
- grad_tokens: bfloat16 [2048, 12288], P('tok', 'hid')
- grad_up_tiles: bfloat16 [6, 256, 24576], P(None, 'tok', 'hid')
- grad_down_tiles: bfloat16 [6, 24576, 256], P(None, ('hid', 'tok'))
- grad_up_left: bfloat16 [12288, 256], P(('hid', 'tok'))
- grad_up_right: bfloat16 [256, 24576], P('tok', 'hid')
- grad_down_left: bfloat16 [24576, 256], P(('hid', 'tok'))
- grad_down_right: bfloat16 [256, 12288], P('tok', 'hid')
Inputs may be any that keep to these rules, and one draw needn't show every extreme that they name: `block_index`: each row names two different sub-blocks.
All inputs are finite; a program needn't handle non-finite values.
Results may differ from a plain program's by a relative error of at most 0.03.
Values may be sent and summed in bfloat16 or wider, within the bound.
No kernel may reach another device: no remote copies, remote signals or barrier semaphores. Data moves between devices by JAX's collectives and lax.ppermute only.
A program may use at most 128 MiB of HBM per device.

v0:
```python
import jax
import jax.numpy as jnp
from jax import lax
from jax.sharding import PartitionSpec as P

GELU_SCALE = 0.7978845608028654
GELU_CUBIC = 0.044715


def partner(block, axis, distance):
    count = lax.axis_size(axis)
    route = []
    for low in range(count):
        high = low | 1 << distance
        if high != low and high < count:
            route += [(low, high), (high, low)]
    return lax.ppermute(block, axis, route)


def gelu_parts(pre_act):
    inner = GELU_SCALE * (pre_act + GELU_CUBIC * pre_act * pre_act * pre_act)
    tanh_value = jnp.tanh(inner)
    value = 0.5 * pre_act * (1.0 + tanh_value)
    slope = 0.5 * (1.0 + tanh_value) + 0.5 * pre_act * (
        1.0 - tanh_value * tanh_value
    ) * GELU_SCALE * (1.0 + 3.0 * GELU_CUBIC * pre_act * pre_act)
    return (value, slope)


def on_device(
    tokens, cotangent, up_tiles, down_tiles, block_index, up_left, up_right, down_left, down_right
):
    hid_count = lax.axis_size("hid")
    level_count = hid_count.bit_length()
    position = lax.axis_index("hid")
    token_rows, feat_width = tokens.shape
    sub_width = feat_width // 3
    block_count = block_index.shape[1]
    hidden_width = up_tiles.shape[2]
    block_width = hidden_width // block_count
    select_float_values = (block_index[..., None] == jnp.arange(3, dtype=jnp.int32)).astype(
        jnp.float32
    )
    select_half_values = select_float_values.astype(jnp.bfloat16)
    up_blocks = [
        up_tiles[partition_key].reshape(2, sub_width, block_count, block_width)
        for partition_key in range(level_count)
    ]
    down_blocks = [
        down_tiles[partition_key].reshape(block_count, block_width, 2, sub_width)
        for partition_key in range(level_count)
    ]

    def partner_of(partition_key):
        if partition_key == 0:
            return position
        return jnp.bitwise_xor(position, jnp.int32(1 << partition_key - 1))

    def choose(field, partition_key):
        reshaped_tiles = field.reshape(token_rows, 3, sub_width)
        return jnp.einsum(
            "rfg,hyf->rhyg",
            reshaped_tiles,
            select_half_values[partition_key],
            preferred_element_type=jnp.float32,
        ).astype(jnp.bfloat16)

    def place(partner_pairs, partition_key):
        placed_blocks = jnp.einsum(
            "kdow,dog->kgw",
            partner_pairs,
            select_float_values[partition_key],
            precision=lax.Precision.HIGHEST,
        )
        return placed_blocks.reshape(token_rows, feat_width).astype(jnp.bfloat16)

    gathered = lax.all_gather(tokens, "hid", axis=1, tiled=True)
    feature_copies = [
        lax.dynamic_slice_in_dim(gathered, partner_of(partition_key) * feat_width, feat_width, 1)
        for partition_key in range(level_count)
    ]
    low_up = lax.psum(
        jnp.dot(tokens, up_left, preferred_element_type=jnp.float32).astype(jnp.bfloat16), "hid"
    )
    chosen_inputs = [
        choose(feature_copies[partition_key], partition_key) for partition_key in range(level_count)
    ]
    pre_act = jnp.dot(low_up, up_right, preferred_element_type=jnp.float32).reshape(
        token_rows, block_count, block_width
    )
    for partition_key in range(level_count):
        pre_act = pre_act + jnp.einsum(
            "tbjs,jsbh->tbh",
            chosen_inputs[partition_key],
            up_blocks[partition_key],
            preferred_element_type=jnp.float32,
        )
    hidden_value, slope = gelu_parts(pre_act)
    hidden_act = hidden_value.astype(jnp.bfloat16)
    hidden_flat = hidden_act.reshape(token_rows, hidden_width)
    low_down = lax.psum(
        jnp.dot(hidden_flat, down_left, preferred_element_type=jnp.float32).astype(jnp.bfloat16),
        "hid",
    )
    out_parts = [
        place(
            jnp.einsum(
                "tbh,bhjs->tbjs",
                hidden_act,
                down_blocks[partition_key],
                preferred_element_type=jnp.float32,
            ),
            partition_key,
        )
        for partition_key in range(level_count)
    ]
    output_acc = out_parts[0].astype(jnp.float32)
    for partition_key in range(1, level_count):
        output_acc = output_acc + partner(
            out_parts[partition_key], "hid", partition_key - 1
        ).astype(jnp.float32)
    layer_out = (
        output_acc + jnp.dot(low_down, down_right, preferred_element_type=jnp.float32)
    ).astype(jnp.bfloat16)
    back_down = lax.psum(
        jnp.dot(cotangent, down_right.T, preferred_element_type=jnp.float32).astype(jnp.bfloat16),
        "hid",
    )
    grad_gathered = lax.all_gather(cotangent, "hid", axis=1, tiled=True)
    grad_copies = [
        lax.dynamic_slice_in_dim(
            grad_gathered, partner_of(partition_key) * feat_width, feat_width, 1
        )
        for partition_key in range(level_count)
    ]
    chosen_grads = [
        choose(grad_copies[partition_key], partition_key) for partition_key in range(level_count)
    ]
    grad_hidden = jnp.dot(back_down, down_left.T, preferred_element_type=jnp.float32).reshape(
        token_rows, block_count, block_width
    )
    for partition_key in range(level_count):
        grad_hidden = grad_hidden + jnp.einsum(
            "tbjs,bhjs->tbh",
            chosen_grads[partition_key],
            down_blocks[partition_key],
            preferred_element_type=jnp.float32,
        )
    down_terms = jnp.stack(
        [
            jnp.einsum(
                "tbh,tbjs->bhjs",
                hidden_act,
                chosen_grads[partition_key],
                preferred_element_type=jnp.float32,
            ).reshape(hidden_width, 2 * sub_width)
            for partition_key in range(level_count)
        ]
    )
    down_left_term = jnp.dot(hidden_flat.T, back_down, preferred_element_type=jnp.float32)
    down_right_term = jnp.dot(low_down.T, cotangent, preferred_element_type=jnp.float32)
    grad_down_tiles, grad_down_left, grad_down_right = (
        lax.psum_scatter(
            down_terms.astype(jnp.bfloat16), "tok", scatter_dimension=1, tiled=True
        ).astype(jnp.float32),
        lax.psum_scatter(
            down_left_term.astype(jnp.bfloat16), "tok", scatter_dimension=0, tiled=True
        ).astype(jnp.float32),
        lax.psum_scatter(
            down_right_term.astype(jnp.bfloat16), "tok", scatter_dimension=0, tiled=True
        ).astype(jnp.float32),
    )
    grad_pre = (grad_hidden * slope).astype(jnp.bfloat16)
    grad_flat = grad_pre.reshape(token_rows, hidden_width)
    back_up = lax.psum(
        jnp.dot(grad_flat, up_right.T, preferred_element_type=jnp.float32).astype(jnp.bfloat16),
        "hid",
    )
    in_parts = [
        place(
            jnp.einsum(
                "tbh,jsbh->tbjs",
                grad_pre,
                up_blocks[partition_key],
                preferred_element_type=jnp.float32,
            ),
            partition_key,
        )
        for partition_key in range(level_count)
    ]
    input_acc = in_parts[0].astype(jnp.float32)
    for partition_key in range(1, level_count):
        input_acc = input_acc + partner(in_parts[partition_key], "hid", partition_key - 1).astype(
            jnp.float32
        )
    grad_tokens = (
        input_acc + jnp.dot(back_up, up_left.T, preferred_element_type=jnp.float32)
    ).astype(jnp.bfloat16)
    up_terms = jnp.stack(
        [
            jnp.einsum(
                "tbjs,tbh->jsbh",
                chosen_inputs[partition_key],
                grad_pre,
                preferred_element_type=jnp.float32,
            ).reshape(2 * sub_width, hidden_width)
            for partition_key in range(level_count)
        ]
    )
    up_right_term = jnp.dot(low_up.T, grad_flat, preferred_element_type=jnp.float32)
    up_left_term = jnp.dot(tokens.T, back_up, preferred_element_type=jnp.float32)
    grad_up_tiles, grad_up_right, grad_up_left = (
        lax.psum_scatter(
            up_terms.astype(jnp.bfloat16), "tok", scatter_dimension=1, tiled=True
        ).astype(jnp.float32),
        lax.psum_scatter(
            up_right_term.astype(jnp.bfloat16), "tok", scatter_dimension=0, tiled=True
        ).astype(jnp.float32),
        lax.psum_scatter(
            up_left_term.astype(jnp.bfloat16), "tok", scatter_dimension=0, tiled=True
        ).astype(jnp.float32),
    )
    return (
        layer_out,
        grad_tokens,
        grad_up_tiles.astype(jnp.bfloat16),
        grad_down_tiles.astype(jnp.bfloat16),
        grad_up_left.astype(jnp.bfloat16),
        grad_up_right.astype(jnp.bfloat16),
        grad_down_left.astype(jnp.bfloat16),
        grad_down_right.astype(jnp.bfloat16),
    )


def solution(mesh):
    return jax.shard_map(
        on_device,
        mesh=mesh,
        in_specs=(
            P("tok", "hid"),
            P("tok", "hid"),
            P(None, None, "hid"),
            P(None, "hid", None),
            P(None, "hid", None),
            P("hid", None),
            P(None, "hid"),
            P("hid", None),
            P(None, "hid"),
        ),
        out_specs=(
            P("tok", "hid"),
            P("tok", "hid"),
            P(None, "tok", "hid"),
            P(None, ("hid", "tok"), None),
            P(("hid", "tok"), None),
            P("tok", "hid"),
            P(("hid", "tok"), None),
            P("tok", "hid"),
        ),
        check_vma=False,
    )
```

profile of v0, /device:TPU:2, one launch (start us, length us, event | category | flops | bytes accessed | tf_op | source)
XLA Modules:
  0.0 776.2 jit_solution(9446525643140161980)
XLA Ops:
  7.3 2.1 convolution_convert_fusion.29
  9.3 1.9 convolution_convert_fusion.31
  16.3 2.2 reshape.191
  18.5 2.1 reshape.190
  20.6 2.3 reshape.189
  25.1 2.5 fusion.172
  30.7 127.4 %all-reduce.7.cloned.1.call-done = (bf16[256,256]{1,0:T(8,128)(2,1)}, bf16[256,256]{1,0:T(8,128)(2,1)}) async-done(((bf16[256,256]{1,0:T(8,128)(2,1)}, bf16[256,256]{1,0:T(8,128)(2,1)}), (bf16[256,256]{1,0:T(8,128)(2,1)}, bf16[256,256]{1,0:T(8,128)(2,1)})) %all-reduce.7.cloned.1.call-update) | async-done | bytes 262160 | tf_op jit(solution)/shard_map/psum | solution.py:82
  158.1 2.1 fusion.175
  160.2 2.2 fusion.176
  162.5 84.4 %all-gather.3.cloned.1.call-done = bf16[256,12288]{0,1:T(8,128)(2,1)} async-done(((bf16[256,384]{0,1:T(8,128)(2,1)}), bf16[256,12288]{0,1:T(8,128)(2,1)}) %all-gather.3.cloned.1.call-update) | async-done | bytes 6291472 | tf_op jit(solution)/shard_map/all_gather | solution.py:77
  246.9 88.8 %all-gather.5.cloned.1.call-done = bf16[256,12288]{0,1:T(8,128)(2,1)} async-done(((bf16[256,384]{0,1:T(8,128)(2,1)}), bf16[256,12288]{0,1:T(8,128)(2,1)}) %all-gather.5.cloned.1.call-update) | async-done | bytes 6291472 | tf_op jit(solution)/shard_map/all_gather | solution.py:129
  335.7 3.0 constant_dynamic-slice_fusion.5
  338.8 1.8 copy.231
  340.5 1.8 copy.225
  344.3 1.8 copy.213
  346.2 1.8 copy.207
  348.0 1.8 copy.280
  349.8 2.0 fusion.14
  351.8 2.0 fusion.20
  353.9 1.8 copy.284
  355.7 2.1 fusion.15
  357.7 2.0 fusion.21
  359.8 1.9 copy.288
  361.6 2.1 fusion.16
  363.7 2.1 fusion.22
  365.8 1.8 copy.292
  367.6 2.1 fusion.17
  369.7 2.1 fusion.23
  371.8 1.8 copy.296
  373.6 2.0 fusion.18
  375.6 2.1 fusion.24
  377.7 1.8 copy.300
  400.2 2.1 copy.346
  404.6 2.0 convolution_convert_fusion.30
  407.3 1.8 constant_dynamic-update-slice_fusion.3
  413.9 4.9 copy.351
  423.4 2.1 fusion.52
  426.2 124.4 %all-reduce.5.cloned.1.call-done = (bf16[256,256]{1,0:T(8,128)(2,1)}, bf16[256,256]{1,0:T(8,128)(2,1)}) async-done(((bf16[256,256]{1,0:T(8,128)(2,1)}, bf16[256,256]{1,0:T(8,128)(2,1)}), (bf16[256,256]{1,0:T(8,128)(2,1)}, bf16[256,256]{1,0:T(8,128)(2,1)})) %all-reduce.5.cloned.1.call-update) | async-done | bytes 262160 | tf_op jit(solution)/shard_map/psum | solution.py:101
  550.5 1.8 fusion.58
  554.2 2.1 convolution_convert_fusion.15
  556.3 1.8 convolution_convert_fusion.26
  558.2 2.0 convolution_convert_fusion.13
  560.2 2.2 fusion.36
  562.7 2.1 convolution_convert_fusion.14
  569.3 2.2 copy.359
  571.6 2.0 stack_reshape.57
  573.6 2.2 copy.361
  575.8 2.0 stack_reshape.58
  577.8 2.2 copy.363
  580.0 2.0 stack_reshape.59
  583.0 2.0 copy.314
  591.1 2.1 collective-permute-start.6
  593.2 1.9 convolution_convert_fusion.12
  595.5 2.1 fusion.50
  599.6 2.5 collective-permute-start.7
  606.1 1.8 constant_dynamic-update-slice_fusion.6
  633.9 3.1 collective-permute-start.2
  637.0 1.8 collective-permute-start.3
  639.6 2.1 add_convert_fusion
  641.7 4.1 collective-permute-done.1
  649.2 10.5 %reduce-scatter.17.cloned.1.call-done = bf16[32,384]{1,0:T(8,128)(2,1)} async-done(((bf16[256,384]{1,0:T(8,128)(2,1)}), bf16[32,384]{1,0:T(8,128)(2,1)}) %reduce-scatter.17.cloned.1.call-update) | async-done | bytes 24592 | tf_op jit(solution)/shard_map/reduce_scatter | solution.py:169
  659.8 35.3 %reduce-scatter.13.cloned.1.call-done = bf16[32,768]{1,0:T(8,128)(2,1)} async-done(((bf16[256,768]{1,0:T(8,128)(2,1)}), bf16[32,768]{1,0:T(8,128)(2,1)}) %reduce-scatter.13.cloned.1.call-update) | async-done | bytes 49168 | tf_op jit(solution)/shard_map/reduce_scatter | solution.py:216
  695.0 35.5 %reduce-scatter.15.cloned.1.call-done = bf16[96,256]{1,0:T(8,128)(2,1)} async-done(((bf16[768,256]{1,0:T(8,128)(2,1)}), bf16[96,256]{1,0:T(8,128)(2,1)}) %reduce-scatter.15.cloned.1.call-update) | async-done | bytes 49168 | tf_op jit(solution)/shard_map/reduce_scatter | solution.py:166
  730.5 38.6 %reduce-scatter.11.cloned.1.call-done = bf16[6,96,256]{2,1,0:T(8,128)(2,1)} async-done(((bf16[6,768,256]{2,1,0:T(8,128)(2,1)}), bf16[6,96,256]{2,1,0:T(8,128)(2,1)}) %reduce-scatter.11.cloned.1.call-update) | async-done | bytes 294928 | tf_op jit(solution)/shard_map/reduce_scatter | solution.py:163
  (273 shorter events, 95.5 us)
Async XLA Ops:
  7.2 150.9 %copy-start = (bf16[256,768]{1,0:T(8,128)(2,1)S(1)}, bf16[256,768]{1,0:T(8,128)(2,1)}, u32[]{:S(2)}) copy-start(bf16[256,768]{1,0:T(8,128)(2,1)} %param.15) | copy-start | bytes 1179652
  7.2 7.8 %copy-start.57 = (s32[6,3,2]{0,2,1:T(2,128)S(1)}, s32[6,3,2]{0,2,1:T(2,128)}, u32[]{:S(2)}) copy-start(s32[6,3,2]{0,2,1:T(2,128)} %param.13) | copy-start | bytes 436
  7.2 7.9 %copy-start.37 = (bf16[6,256,768]{2,1,0:T(8,128)(2,1)S(1)}, bf16[6,256,768]{2,1,0:T(8,128)(2,1)}, u32[]{:S(2)}) copy-start(bf16[6,256,768]{2,1,0:T(8,128)(2,1)} %param.11) | copy-start | bytes 7077892
  7.2 150.9 %all-reduce.7.cloned.1.call-start = ((), (), s32[]{:S(2)}) async-start(), calls=%async_computation.15 | async-start | bytes 524288 | tf_op jit(solution)/shard_map/psum | solution.py:82
  11.3 235.6 %all-gather.3.cloned.1.call-start = ((), (), s32[]{:S(2)}) async-start(), calls=%async_computation.6 | async-start | bytes 6488064 | tf_op jit(solution)/shard_map/all_gather | solution.py:77
  13.1 322.6 %all-gather.5.cloned.1.call-start = ((), (), s32[]{:S(2)}) async-start(), calls=%async_computation.7 | async-start | bytes 6488064 | tf_op jit(solution)/shard_map/all_gather | solution.py:129
  14.9 535.6 %all-reduce.5.cloned.1.call-start = ((), (), s32[]{:S(2)}) async-start(), calls=%async_computation.14 | async-start | bytes 524288 | tf_op jit(solution)/shard_map/psum | solution.py:101
  16.3 6.6 copy-start.41
  23.1 360.5 %copy-start.10 = (bf16[2,128,3,256]{3,2,1,0:T(4,128)(2,1)}, bf16[2,128,3,256]{3,2,1,0:T(4,128)(2,1)S(1)}, u32[]{:S(2)}) copy-start(bf16[2,128,3,256]{3,2,1,0:T(4,128)(2,1)S(1)} %reshape.192) | copy-start | bytes 1179652
  27.9 356.9 %copy-start.2 = (bf16[3,256,2,128]{3,2,1,0:T(2,128)(2,1)}, bf16[3,256,2,128]{3,2,1,0:T(2,128)(2,1)S(1)}, u32[]{:S(2)}) copy-start(bf16[3,256,2,128]{3,2,1,0:T(2,128)(2,1)S(1)} %reshape_squeeze.46) | copy-start | bytes 1179652
  28.0 357.1 %copy-start.4 = (bf16[3,256,2,128]{3,2,1,0:T(2,128)(2,1)}, bf16[3,256,2,128]{3,2,1,0:T(2,128)(2,1)S(1)}, u32[]{:S(2)}) copy-start(bf16[3,256,2,128]{3,2,1,0:T(2,128)(2,1)S(1)} %reshape_squeeze.45) | copy-start | bytes 1179652
  28.1 357.4 %copy-start.6 = (bf16[3,256,2,128]{3,2,1,0:T(2,128)(2,1)}, bf16[3,256,2,128]{3,2,1,0:T(2,128)(2,1)S(1)}, u32[]{:S(2)}) copy-start(bf16[3,256,2,128]{3,2,1,0:T(2,128)(2,1)S(1)} %reshape_squeeze.44) | copy-start | bytes 1179652
  28.2 357.7 %copy-start.8 = (bf16[3,256,2,128]{3,2,1,0:T(2,128)(2,1)}, bf16[3,256,2,128]{3,2,1,0:T(2,128)(2,1)S(1)}, u32[]{:S(2)}) copy-start(bf16[3,256,2,128]{3,2,1,0:T(2,128)(2,1)S(1)} %reshape_squeeze.43) | copy-start | bytes 1179652
  359.8 13.8 %copy-start.56 = (bf16[3,2,3,1]{2,1,0,3:T(2,128)(2,1)S(1)}, bf16[3,2,3,1]{2,1,0,3:T(2,128)(2,1)}, u32[]{:S(2)}) copy-start(bf16[3,2,3,1]{2,1,0,3:T(2,128)(2,1)} %get-tuple-element.77) | copy-start | bytes 112
  365.8 13.7 %copy-start.55 = (bf16[3,2,3,1]{2,1,0,3:T(2,128)(2,1)S(1)}, bf16[3,2,3,1]{2,1,0,3:T(2,128)(2,1)}, u32[]{:S(2)}) copy-start(bf16[3,2,3,1]{2,1,0,3:T(2,128)(2,1)} %get-tuple-element.76) | copy-start | bytes 112
  379.5 3.5 copy-start.13
  379.5 3.5 copy-start.33
  379.5 3.8 copy-start.15
  379.5 3.8 copy-start.32
  381.2 3.3 copy-start.23
  388.8 3.4 copy-start.34
  404.6 5.4 copy-start.48
  409.2 238.3 %reduce-scatter.9.cloned.1.call-start = ((), (), s32[]{:S(2)}) async-start(), calls=%async_computation.8 | async-start | bytes 3538944 | tf_op jit(solution)/shard_map/reduce_scatter | solution.py:213
  418.8 4.2 copy-start.18
  418.8 230.4 %reduce-scatter.19.cloned.1.call-start = ((), (), s32[]{:S(2)}) async-start(), calls=%async_computation.13 | async-start | bytes 221184
  418.9 3.1 copy-start.30
  420.9 4.6 copy-start.20
  423.4 127.2 %copy-start.39 = (bf16[256,384]{1,0:T(8,128)(2,1)S(1)}, bf16[256,384]{1,0:T(8,128)(2,1)}, u32[]{:S(2)}) copy-start(bf16[256,384]{1,0:T(8,128)(2,1)} %param.9) | copy-start | bytes 589828
  425.5 130.8 %copy-start.40 = (bf16[256,384]{1,0:T(8,128)(2,1)S(1)}, bf16[256,384]{1,0:T(8,128)(2,1)}, u32[]{:S(2)}) copy-start(bf16[256,384]{1,0:T(8,128)(2,1)} %param.10) | copy-start | bytes 589828
  554.1 105.6 %reduce-scatter.17.cloned.1.call-start = ((), (), s32[]{:S(2)}) async-start(), calls=%async_computation.12 | async-start | bytes 221184 | tf_op jit(solution)/shard_map/reduce_scatter | solution.py:169
  558.2 6.7 copy-start.47
  558.2 136.9 %reduce-scatter.13.cloned.1.call-start = ((), (), s32[]{:S(2)}) async-start(), calls=%async_computation.10 | async-start | bytes 442368 | tf_op jit(solution)/shard_map/reduce_scatter | solution.py:216
  562.5 5.4 copy-start.46
  562.5 168.0 %reduce-scatter.15.cloned.1.call-start = ((), (), s32[]{:S(2)}) async-start(), calls=%async_computation.11 | async-start | bytes 442368 | tf_op jit(solution)/shard_map/reduce_scatter | solution.py:166
  569.3 12.7 %copy-start.38 = (f32[256,3,128]{2,1,0:T(4,128)S(1)}, f32[256,3,128]{2,1,0:T(4,128)}, u32[]{:S(2)}) copy-start(f32[256,3,128]{2,1,0:T(4,128)} %fusion.36) | copy-start | bytes 1179652
  573.6 11.4 %copy-start.50 = (bf16[256,3,128]{2,1,0:T(4,128)(2,1)S(1)}, bf16[256,3,128]{2,1,0:T(4,128)(2,1)}, u32[]{:S(2)}) copy-start(bf16[256,3,128]{2,1,0:T(4,128)(2,1)} %fusion.52) | copy-start | bytes 589828
  583.0 12.1 %copy-start.14 = (bf16[2,128,3,256]{3,2,1,0:T(4,128)(2,1)S(1)}, bf16[2,128,3,256]{3,2,1,0:T(4,128)(2,1)}, u32[]{:S(2)}) copy-start(bf16[2,128,3,256]{3,2,1,0:T(4,128)(2,1)} %reshape.190) | copy-start | bytes 1179652
  587.6 44.5 %collective-permute-start.5 = (bf16[256,384]{1,0:T(8,128)(2,1)}, bf16[256,384]{1,0:T(8,128)(2,1)}, u32[]{:S(2)}, u32[]{:S(2)}) collective-permute-start(bf16[256,384]{1,0:T(8,128)(2,1)} %copy.313), channel_id=1, source_target_pairs={{0,8},{8,0},{16,24},{24,16},{32,40},{40,32},{48,56},{56,48},{64,72... | collective-permute-start | bytes 589832 | tf_op jit(solution)/shard_map/ppermute | solution.py:17
  591.1 41.5 %collective-permute-start.6 = (bf16[256,384]{1,0:T(8,128)(2,1)}, bf16[256,384]{1,0:T(8,128)(2,1)}, u32[]{:S(2)}, u32[]{:S(2)}) collective-permute-start(bf16[256,384]{1,0:T(8,128)(2,1)} %copy.320), channel_id=1, source_target_pairs={{0,16},{16,0},{8,24},{24,8},{32,48},{48,32},{40,56},{56,40},{64,80... | collective-permute-start | bytes 589832 | tf_op jit(solution)/shard_map/ppermute | solution.py:17
  595.4 7.5 copy-start.42
  595.4 8.3 %copy-start.43 = (bf16[1,768,256]{2,1,0:T(8,128)(2,1)S(1)}, bf16[1,768,256]{2,1,0:T(8,128)(2,1)}, u32[]{:S(2)}) copy-start(bf16[1,768,256]{2,1,0:T(8,128)(2,1)} %stack_reshape.56) | copy-start | bytes 1179652
  595.4 173.7 %reduce-scatter.11.cloned.1.call-start = ((), (), s32[]{:S(2)}) async-start(), calls=%async_computation.9 | async-start | bytes 2654208 | tf_op jit(solution)/shard_map/reduce_scatter | solution.py:163
  599.6 4.9 copy-start.44
  599.6 5.7 copy-start.45
  599.6 34.3 %collective-permute-start.7 = (bf16[256,384]{1,0:T(8,128)(2,1)}, bf16[256,384]{1,0:T(8,128)(2,1)}, u32[]{:S(2)}, u32[]{:S(2)}) collective-permute-start(bf16[256,384]{1,0:T(8,128)(2,1)} %copy.326), channel_id=1, source_target_pairs={{0,32},{32,0},{8,40},{40,8},{16,48},{48,16},{24,56},{56,24},{64,96... | collective-permute-start | bytes 589832 | tf_op jit(solution)/shard_map/ppermute | solution.py:17
  604.5 3.4 copy-start.12
  607.9 3.9 copy-start.11
  610.0 26.9 %collective-permute-start.8 = (bf16[256,384]{1,0:T(8,128)(2,1)S(1)}, bf16[256,384]{1,0:T(8,128)(2,1)S(1)}, u32[]{:S(2)}, u32[]{:S(2)}) collective-permute-start(bf16[256,384]{1,0:T(8,128)(2,1)S(1)} %copy.332), channel_id=1, source_target_pairs={{0,64},{64,0},{8,72},{72,8},{16,80},{80,16},{24,88},{88,24},{32,96... | collective-permute-start | bytes 589832 | tf_op jit(solution)/shard_map/ppermute | solution.py:17
  614.5 3.6 copy-start.9
  614.6 24.2 %collective-permute-start.9 = (bf16[256,384]{1,0:T(8,128)(2,1)}, bf16[256,384]{1,0:T(8,128)(2,1)S(1)}, u32[]{:S(2)}, u32[]{:S(2)}) collective-permute-start(bf16[256,384]{1,0:T(8,128)(2,1)} %copy.338), channel_id=1, source_target_pairs={{0,128},{128,0},{8,136},{136,8},{16,144},{144,16},{24,152},{152,24... | collective-permute-start | bytes 589832 | tf_op jit(solution)/shard_map/ppermute | solution.py:17
  618.0 3.0 copy-start.7
  619.9 3.8 copy-start.5
  622.7 3.8 copy-start.3
  628.2 11.4 %copy-start.49 = (f32[256,384]{1,0:T(8,128)S(1)}, f32[256,384]{1,0:T(8,128)}, u32[]{:S(2)}) copy-start(f32[256,384]{1,0:T(8,128)} %copy.314) | copy-start | bytes 1179652
  628.2 11.4 %copy-start.51 = (bf16[384,256]{1,0:T(8,128)(2,1)S(1)}, bf16[384,256]{1,0:T(8,128)(2,1)}, u32[]{:S(2)}) copy-start(bf16[384,256]{1,0:T(8,128)(2,1)} %param.14) | copy-start | bytes 589828
  628.2 11.4 %copy-start.54 = (bf16[256,256]{1,0:T(8,128)(2,1)S(1)}, bf16[256,256]{1,0:T(8,128)(2,1)}, u32[]{:S(2)}) copy-start(bf16[256,256]{1,0:T(8,128)(2,1)} %get-tuple-element.33) | copy-start | bytes 393220
  629.5 17.0 %copy-start.52 = (bf16[256,384]{1,0:T(8,128)(2,1)S(1)}, bf16[256,384]{1,0:T(8,128)(2,1)}, u32[]{:S(2)}) copy-start(bf16[256,384]{1,0:T(8,128)(2,1)} %param.17) | copy-start | bytes 589828
  629.6 17.0 %copy-start.53 = (bf16[256,256]{1,0:T(8,128)(2,1)S(1)}, bf16[256,256]{1,0:T(8,128)(2,1)}, u32[]{:S(2)}) copy-start(bf16[256,256]{1,0:T(8,128)(2,1)} %get-tuple-element.32) | copy-start | bytes 393220
  631.2 137.9 %copy-start.1 = (bf16[256,768]{1,0:T(8,128)(2,1)S(1)}, bf16[256,768]{1,0:T(8,128)(2,1)}, u32[]{:S(2)}) copy-start(bf16[256,768]{1,0:T(8,128)(2,1)} %param.15) | copy-start | bytes 1179652
  632.0 9.7 %collective-permute-start = (bf16[256,384]{1,0:T(8,128)(2,1)}, bf16[256,384]{1,0:T(8,128)(2,1)S(1)}, u32[]{:S(2)}, u32[]{:S(2)}) collective-permute-start(bf16[256,384]{1,0:T(8,128)(2,1)} %copy.251), channel_id=1, source_target_pairs={{0,8},{8,0},{16,24},{24,16},{32,40},{40,32},{48,56},{56,48},{64,72... | collective-permute-start | bytes 589832 | tf_op jit(solution)/shard_map/ppermute | solution.py:17
  632.6 13.2 %collective-permute-start.1 = (bf16[256,384]{1,0:T(8,128)(2,1)}, bf16[256,384]{1,0:T(8,128)(2,1)S(1)}, u32[]{:S(2)}, u32[]{:S(2)}) collective-permute-start(bf16[256,384]{1,0:T(8,128)(2,1)} %copy.258), channel_id=1, source_target_pairs={{0,16},{16,0},{8,24},{24,8},{32,48},{48,32},{40,56},{56,40},{64,80... | collective-permute-start | bytes 589832 | tf_op jit(solution)/shard_map/ppermute | solution.py:17
  633.9 12.6 %collective-permute-start.2 = (bf16[256,384]{1,0:T(8,128)(2,1)}, bf16[256,384]{1,0:T(8,128)(2,1)S(1)}, u32[]{:S(2)}, u32[]{:S(2)}) collective-permute-start(bf16[256,384]{1,0:T(8,128)(2,1)} %copy.264), channel_id=1, source_target_pairs={{0,32},{32,0},{8,40},{40,8},{16,48},{48,16},{24,56},{56,24},{64,96... | collective-permute-start | bytes 589832 | tf_op jit(solution)/shard_map/ppermute | solution.py:17
  637.0 9.6 %collective-permute-start.3 = (bf16[256,384]{1,0:T(8,128)(2,1)}, bf16[256,384]{1,0:T(8,128)(2,1)S(1)}, u32[]{:S(2)}, u32[]{:S(2)}) collective-permute-start(bf16[256,384]{1,0:T(8,128)(2,1)} %copy.270), channel_id=1, source_target_pairs={{0,64},{64,0},{8,72},{72,8},{16,80},{80,16},{24,88},{88,24},{32,96... | collective-permute-start | bytes 589832 | tf_op jit(solution)/shard_map/ppermute | solution.py:17
  638.7 7.8 %collective-permute-start.4 = (bf16[256,384]{1,0:T(8,128)(2,1)}, bf16[256,384]{1,0:T(8,128)(2,1)S(1)}, u32[]{:S(2)}, u32[]{:S(2)}) collective-permute-start(bf16[256,384]{1,0:T(8,128)(2,1)} %copy.276), channel_id=1, source_target_pairs={{0,128},{128,0},{8,136},{136,8},{16,144},{144,16},{24,152},{152,24... | collective-permute-start | bytes 589832 | tf_op jit(solution)/shard_map/ppermute | solution.py:17
  (14 other events, 19.0 us)
Sparse Core Ops, SparseCore 0:
  12.1 145.9 all-reduce.6
  161.3 85.5 all-gather.2
  250.0 85.6 all-gather.4
  409.3 141.2 all-reduce.4
  552.9 36.3 reduce-scatter.8
  592.3 32.1 reduce-scatter.18
  627.7 32.0 reduce-scatter.16
  662.8 32.1 reduce-scatter.12
  698.3 32.1 reduce-scatter.14
  733.5 35.5 reduce-scatter.10
where the time goes:
time: 781 us; the launch traced here: 776 us
  waiting for transfers between devices  550 us (70%)
  local copies, waits for them, and re-layouts  106 us (14%)
  matrix products  87.5 us (11%)
  starting transfers between devices  17 us (2%)
  between operations  15.4 us (2%)
    psum x1, waiting for transfers between devices, on_device(): lax.psum(jnp.dot(tokens, up_left, preferred_element_type=jnp.float32).ast...  127 us
    psum x1, waiting for transfers between devices, on_device(): lax.psum(jnp.dot(hidden_flat, down_left, preferred_element_type=jnp.float...  124 us
    all_gather x1, waiting for transfers between devices, on_device(): grad_gathered = lax.all_gather(cotangent, 'hid', axis=1, tiled=True)  88.8 us
    all_gather x1, waiting for transfers between devices, on_device(): gathered = lax.all_gather(tokens, 'hid', axis=1, tiled=True)  84.4 us
    reduce_scatter x1, waiting for transfers between devices, on_device(): lax.psum_scatter(down_terms.astype(jnp.bfloat16), 'tok', scatter_dimensio...  38.6 us
    reduce_scatter x1, waiting for transfers between devices, on_device(): lax.psum_scatter(down_left_term.astype(jnp.bfloat16), 'tok', scatter_dime...  35.5 us
    reduce_scatter x1, waiting for transfers between devices, on_device(): lax.psum_scatter(up_right_term.astype(jnp.bfloat16), 'tok', scatter_dimen...  35.3 us
    dot_general x12, matrix products, choose(): jnp.einsum('rfg,hyf->rhyg', reshaped_tiles, select_half_values[partition_...  22.3 us
  transfers between devices with their start and end apart: 20, of which 10 were waited for; matrix products, arithmetic and copies ran while one was open for 15% of the time, Pallas kernels for 0%

commit v1 on v0

--- a/solution.py
+++ b/solution.py
@@ -98,9 +98,13 @@
     hidden_value, slope = gelu_parts(pre_act)
     hidden_act = hidden_value.astype(jnp.bfloat16)
     hidden_flat = hidden_act.reshape(token_rows, hidden_width)
-    low_down = lax.psum(
-        jnp.dot(hidden_flat, down_left, preferred_element_type=jnp.float32).astype(jnp.bfloat16),
-        "hid",
+
+    def lane_open(in_array):
+        outcome_arr = jax.lax.all_gather(in_array, "hid").sum(axis=0)
+        return outcome_arr
+
+    low_down = lane_open(
+        jnp.dot(hidden_flat, down_left, preferred_element_type=jnp.float32).astype(jnp.bfloat16)
     )
     out_parts = [
         place(

time: 781 us -> 852 us (1.091)
  waiting for transfers between devices: 550 us -> 614 us
  starting transfers between devices: 17 us -> 29.4 us
  matrix products: 87.5 us -> 77.8 us
    unnamed x11 -> x12, waiting for transfers between devices: 0.17 us -> 31.6 us
    psum x1, waiting for transfers between devices: 124 us -> 99.4 us  [on_device(): lax.psum(jnp.dot(grad_flat, up_right.T, preferred_element_type=jnp.float3...]
    reduce_scatter x1, waiting for transfers between devices: 0.01 us -> 24.6 us  [on_device(): lax.psum_scatter(up_terms.astype(jnp.bfloat16), 'tok', scatter_dimension=...]
    reduce_scatter x1, waiting for transfers between devices: 10.5 us -> 35 us  [on_device(): lax.psum_scatter(down_right_term.astype(jnp.bfloat16), 'tok', scatter_dim...]
    reduce_scatter x1, starting transfers between devices: 0.04 us -> 11.5 us  [on_device(): lax.psum_scatter(up_right_term.astype(jnp.bfloat16), 'tok', scatter_dimen...]
    all_gather x0 -> x1, waiting for transfers between devices: none -> 10.7 us  [lane_open(): outcome_arr = jax.lax.all_gather(in_array, 'hid').sum(axis=0)]
    unnamed x131 -> x139, local copies, waits for them, and re-layouts: 17.7 us -> 18.9 us
  transfers between devices with their start and end apart: 20 -> 21, of which waited for: 10 -> 11; matrix products, arithmetic and copies ran while one was open for 15% -> 15% of each run, Pallas kernels for 0% -> 0%
where the time goes in v1:
time: 852 us; the launch traced here: 841 us
  waiting for transfers between devices  614 us (72%)
  local copies, waits for them, and re-layouts  101 us (12%)
  matrix products  77.8 us (9%)
  starting transfers between devices  29.4 us (3%)
  between operations  15.4 us (2%)
    psum x1, waiting for transfers between devices, on_device(): lax.psum(jnp.dot(tokens, up_left, preferred_element_type=jnp.float32).ast...  131 us
    psum x1, waiting for transfers between devices, on_device(): lax.psum(jnp.dot(grad_flat, up_right.T, preferred_element_type=jnp.float3...  99.4 us
    all_gather x1, waiting for transfers between devices, on_device(): grad_gathered = lax.all_gather(cotangent, 'hid', axis=1, tiled=True)  88.8 us
    all_gather x1, waiting for transfers between devices, on_device(): gathered = lax.all_gather(tokens, 'hid', axis=1, tiled=True)  84.4 us
    reduce_scatter x1, waiting for transfers between devices, on_device(): lax.psum_scatter(down_terms.astype(jnp.bfloat16), 'tok', scatter_dimensio...  38.6 us
    reduce_scatter x1, waiting for transfers between devices, on_device(): lax.psum_scatter(down_left_term.astype(jnp.bfloat16), 'tok', scatter_dime...  35.4 us
    reduce_scatter x1, waiting for transfers between devices, on_device(): lax.psum_scatter(up_right_term.astype(jnp.bfloat16), 'tok', scatter_dimen...  35.2 us
    reduce_scatter x1, waiting for transfers between devices, on_device(): lax.psum_scatter(down_right_term.astype(jnp.bfloat16), 'tok', scatter_dim...  35 us
  transfers between devices with their start and end apart: 21, of which 11 were waited for; matrix products, arithmetic and copies ran while one was open for 15% of the time, Pallas kernels for 0%

profile of v1, /device:TPU:2, one launch (start us, length us, event | category | flops | bytes accessed | tf_op | source)
XLA Modules:
  0.0 841.1 jit_solution(6058491705306170514)
XLA Ops:
  7.2 2.0 convolution_convert_fusion.29
  9.2 1.9 convolution_convert_fusion.31
  11.2 1.7 copy.205
  13.0 1.7 copy.278
  15.0 1.7 fusion.173
  21.8 2.5 fusion.172
  27.4 130.7 %all-reduce.6.cloned.1.call-done = (bf16[256,256]{1,0:T(8,128)(2,1)}, bf16[256,256]{1,0:T(8,128)(2,1)}) async-done(((bf16[256,256]{1,0:T(8,128)(2,1)}, bf16[256,256]{1,0:T(8,128)(2,1)}), (bf16[256,256]{1,0:T(8,128)(2,1)}, bf16[256,256]{1,0:T(8,128)(2,1)})) %all-reduce.6.cloned.1.call-update) | async-done | bytes 262160 | tf_op jit(solution)/shard_map/psum | solution.py:82
  158.1 2.1 fusion.175
  160.2 2.3 fusion.176
  162.4 84.4 %all-gather.5.cloned.1.call-done = bf16[256,12288]{0,1:T(8,128)(2,1)} async-done(((bf16[256,384]{0,1:T(8,128)(2,1)}), bf16[256,12288]{0,1:T(8,128)(2,1)}) %all-gather.5.cloned.1.call-update) | async-done | bytes 6291472 | tf_op jit(solution)/shard_map/all_gather | solution.py:77
  246.8 88.8 %all-gather.7.cloned.1.call-done = bf16[256,12288]{0,1:T(8,128)(2,1)} async-done(((bf16[256,384]{0,1:T(8,128)(2,1)}), bf16[256,12288]{0,1:T(8,128)(2,1)}) %all-gather.7.cloned.1.call-update) | async-done | bytes 6291472 | tf_op jit(solution)/shard_map/all_gather | solution.py:133
  335.7 3.0 constant_dynamic-slice_fusion.5
  338.7 1.8 copy.231
  340.5 1.8 copy.225
  344.3 1.8 copy.213
  346.1 1.8 copy.207
  347.9 1.8 copy.280
  349.7 2.0 fusion.14
  351.7 2.1 fusion.20
  353.8 1.8 copy.284
  355.6 2.1 fusion.15
  357.7 2.0 fusion.21
  359.7 1.8 copy.288
  361.5 2.1 fusion.16
  363.6 2.1 fusion.22
  365.7 1.8 copy.292
  367.5 2.1 fusion.17
  369.6 2.1 fusion.23
  371.7 1.8 copy.296
  373.5 2.0 fusion.18
  375.5 2.0 fusion.24
  377.5 1.8 copy.300
  379.7 1.6 fusion.25
  381.3 1.7 convolution_bitcast_fusion.19
  390.2 2.0 convolution_convert_fusion.30
  396.4 2.0 stack_reshape.49
  399.9 2.0 stack_reshape.50
  403.3 2.1 stack_reshape.51
  406.8 2.0 stack_reshape.52
  410.3 2.0 stack_reshape.53
  417.0 4.9 copy.351
  429.9 99.4 %all-reduce.4.cloned.1.call-done = bf16[256,256]{1,0:T(8,128)(2,1)} async-done(((bf16[256,256]{1,0:T(8,128)(2,1)}), bf16[256,256]{1,0:T(8,128)(2,1)}) %all-reduce.4.cloned.1.call-update) | async-done | bytes 131088 | tf_op jit(solution)/shard_map/psum | solution.py:179
  531.3 11.5 %reduce-scatter.13.cloned.1.call-start = ((), (), s32[]{:S(2)}) async-start(), calls=%async_computation.11 | async-start | bytes 442368 | tf_op jit(solution)/shard_map/reduce_scatter | solution.py:220
  545.4 1.8 constant_dynamic-update-slice_fusion.11
  555.1 1.9 copy.314
  559.3 1.8 constant_dynamic-update-slice_fusion.10
  561.1 1.8 constant_dynamic-update-slice_fusion.9
  562.9 1.9 convolution_convert_fusion.12
  578.0 2.5 collective-permute-start.7
  586.1 2.5 collective-permute-start.9
  604.5 10.7 %all-gather.9.cloned.1.call-done = bf16[8192,256]{1,0:T(8,128)(2,1)} async-done(((bf16[256,256]{1,0:T(8,128)(2,1)}), bf16[8192,256]{1,0:T(8,128)(2,1)}) %all-gather.9.cloned.1.call-update) | async-done | bytes 4194320 | tf_op jit(solution)/shard_map/all_gather | solution.py:103
  615.3 2.9 reduce_sum.12
  620.5 1.9 collective-permute-start.1
  622.4 2.8 collective-permute-start.2
  626.3 2.1 collective-permute-start.4
  628.4 2.0 add_convert_fusion
  630.3 24.6 %reduce-scatter.9.cloned.1.call-done = bf16[6,32,768]{2,0,1:T(8,128)(2,1)} async-done(((bf16[6,256,768]{2,0,1:T(8,128)(2,1)}), bf16[6,32,768]{2,0,1:T(8,128)(2,1)}) %reduce-scatter.9.cloned.1.call-update) | async-done | bytes 294928 | tf_op jit(solution)/shard_map/reduce_scatter | solution.py:217
  654.9 1.8 copy.364
  656.7 1.8 add_convert_fusion.1
  658.6 31.4 %reduce-scatter.19.cloned.1.call-done = bf16[48,256]{1,0:T(8,128)(2,1)} async-done(((bf16[384,256]{1,0:T(8,128)(2,1)}), bf16[48,256]{1,0:T(8,128)(2,1)}) %reduce-scatter.19.cloned.1.call-update) | async-done | bytes 24592
  689.9 35.2 %reduce-scatter.13.cloned.1.call-done = bf16[32,768]{1,0:T(8,128)(2,1)} async-done(((bf16[256,768]{1,0:T(8,128)(2,1)}), bf16[32,768]{1,0:T(8,128)(2,1)}) %reduce-scatter.13.cloned.1.call-update) | async-done | bytes 49168 | tf_op jit(solution)/shard_map/reduce_scatter | solution.py:220
  725.1 35.4 %reduce-scatter.15.cloned.1.call-done = bf16[96,256]{1,0:T(8,128)(2,1)} async-done(((bf16[768,256]{1,0:T(8,128)(2,1)}), bf16[96,256]{1,0:T(8,128)(2,1)}) %reduce-scatter.15.cloned.1.call-update) | async-done | bytes 49168 | tf_op jit(solution)/shard_map/reduce_scatter | solution.py:170
  760.6 38.6 %reduce-scatter.11.cloned.1.call-done = bf16[6,96,256]{2,1,0:T(8,128)(2,1)} async-done(((bf16[6,768,256]{2,1,0:T(8,128)(2,1)}), bf16[6,96,256]{2,1,0:T(8,128)(2,1)}) %reduce-scatter.11.cloned.1.call-update) | async-done | bytes 294928 | tf_op jit(solution)/shard_map/reduce_scatter | solution.py:167
  799.2 35.0 %reduce-scatter.17.cloned.1.call-done = bf16[32,384]{1,0:T(8,128)(2,1)} async-done(((bf16[256,384]{1,0:T(8,128)(2,1)}), bf16[32,384]{1,0:T(8,128)(2,1)}) %reduce-scatter.17.cloned.1.call-update) | async-done | bytes 24592 | tf_op jit(solution)/shard_map/reduce_scatter | solution.py:173
  (285 shorter events, 92.8 us)
Async XLA Ops:
  7.2 150.9 %copy-start = (bf16[256,768]{1,0:T(8,128)(2,1)S(1)}, bf16[256,768]{1,0:T(8,128)(2,1)}, u32[]{:S(2)}) copy-start(bf16[256,768]{1,0:T(8,128)(2,1)} %param.15) | copy-start | bytes 1179652
  7.2 7.7 copy-start.61
  7.2 150.9 %all-reduce.6.cloned.1.call-start = ((), (), s32[]{:S(2)}) async-start(), calls=%async_computation.16 | async-start | bytes 524288 | tf_op jit(solution)/shard_map/psum | solution.py:82
  11.1 235.7 %all-gather.5.cloned.1.call-start = ((), (), s32[]{:S(2)}) async-start(), calls=%async_computation.6 | async-start | bytes 6488064 | tf_op jit(solution)/shard_map/all_gather | solution.py:77
  13.0 322.7 %all-gather.7.cloned.1.call-start = ((), (), s32[]{:S(2)}) async-start(), calls=%async_computation.7 | async-start | bytes 6488064 | tf_op jit(solution)/shard_map/all_gather | solution.py:133
  14.8 514.5 %all-reduce.4.cloned.1.call-start = ((), (), s32[]{:S(2)}) async-start(), calls=%async_computation.8 | async-start | bytes 262144 | tf_op jit(solution)/shard_map/psum | solution.py:179
  19.8 363.9 %copy-start.10 = (bf16[2,128,3,256]{3,2,1,0:T(4,128)(2,1)}, bf16[2,128,3,256]{3,2,1,0:T(4,128)(2,1)S(1)}, u32[]{:S(2)}) copy-start(bf16[2,128,3,256]{3,2,1,0:T(4,128)(2,1)S(1)} %reshape.193) | copy-start | bytes 1179652
  24.5 360.3 %copy-start.2 = (bf16[3,256,2,128]{3,2,1,0:T(2,128)(2,1)}, bf16[3,256,2,128]{3,2,1,0:T(2,128)(2,1)S(1)}, u32[]{:S(2)}) copy-start(bf16[3,256,2,128]{3,2,1,0:T(2,128)(2,1)S(1)} %reshape_squeeze.46) | copy-start | bytes 1179652
  24.7 360.6 %copy-start.4 = (bf16[3,256,2,128]{3,2,1,0:T(2,128)(2,1)}, bf16[3,256,2,128]{3,2,1,0:T(2,128)(2,1)S(1)}, u32[]{:S(2)}) copy-start(bf16[3,256,2,128]{3,2,1,0:T(2,128)(2,1)S(1)} %reshape_squeeze.45) | copy-start | bytes 1179652
  24.8 360.9 %copy-start.6 = (bf16[3,256,2,128]{3,2,1,0:T(2,128)(2,1)}, bf16[3,256,2,128]{3,2,1,0:T(2,128)(2,1)S(1)}, u32[]{:S(2)}) copy-start(bf16[3,256,2,128]{3,2,1,0:T(2,128)(2,1)S(1)} %reshape_squeeze.44) | copy-start | bytes 1179652
  24.9 361.1 %copy-start.8 = (bf16[3,256,2,128]{3,2,1,0:T(2,128)(2,1)}, bf16[3,256,2,128]{3,2,1,0:T(2,128)(2,1)S(1)}, u32[]{:S(2)}) copy-start(bf16[3,256,2,128]{3,2,1,0:T(2,128)(2,1)S(1)} %reshape_squeeze.43) | copy-start | bytes 1179652
  359.7 13.7 %copy-start.60 = (bf16[3,2,3,1]{2,1,0,3:T(2,128)(2,1)S(1)}, bf16[3,2,3,1]{2,1,0,3:T(2,128)(2,1)}, u32[]{:S(2)}) copy-start(bf16[3,2,3,1]{2,1,0,3:T(2,128)(2,1)} %get-tuple-element.75) | copy-start | bytes 112
  365.7 13.7 %copy-start.59 = (bf16[3,2,3,1]{2,1,0,3:T(2,128)(2,1)S(1)}, bf16[3,2,3,1]{2,1,0,3:T(2,128)(2,1)}, u32[]{:S(2)}) copy-start(bf16[3,2,3,1]{2,1,0,3:T(2,128)(2,1)} %get-tuple-element.74) | copy-start | bytes 112
  379.3 3.7 copy-start.13
  379.3 3.7 copy-start.37
  379.3 4.0 copy-start.14
  379.3 4.0 copy-start.35
  379.7 4.0 copy-start.40
  388.1 4.1 copy-start.22
  388.9 6.1 copy-start.34
  390.2 225.1 %all-gather.9.cloned.1.call-start = ((), (), s32[]{:S(2)}) async-start(), calls=%async_computation.14 | async-start | bytes 4325376 | tf_op jit(solution)/shard_map/all_gather | solution.py:103
  392.2 262.7 %reduce-scatter.9.cloned.1.call-start = ((), (), s32[]{:S(2)}) async-start(), calls=%async_computation.9 | async-start | bytes 3538944 | tf_op jit(solution)/shard_map/reduce_scatter | solution.py:217
  392.5 5.9 copy-start.36
  395.3 6.6 copy-start.38
  398.7 6.6 copy-start.39
  402.1 6.7 copy-start.41
  406.8 6.3 copy-start.47
  409.1 4.8 copy-start.48
  412.3 4.0 copy-start.51
  422.0 268.0 %reduce-scatter.19.cloned.1.call-start = ((), (), s32[]{:S(2)}) async-start(), calls=%async_computation.15 | async-start | bytes 221184
  423.7 4.1 copy-start.17
  425.8 3.8 copy-start.19
  427.8 101.5 %copy-start.44 = (bf16[256,384]{1,0:T(8,128)(2,1)S(1)}, bf16[256,384]{1,0:T(8,128)(2,1)}, u32[]{:S(2)}) copy-start(bf16[256,384]{1,0:T(8,128)(2,1)} %param.9) | copy-start | bytes 589828
  428.1 114.7 %copy-start.57 = (bf16[256,256]{1,0:T(8,128)(2,1)S(1)}, bf16[256,256]{1,0:T(8,128)(2,1)}, u32[]{:S(2)}) copy-start(bf16[256,256]{1,0:T(8,128)(2,1)} %get-tuple-element.32) | copy-start | bytes 393220
  531.3 193.9 %reduce-scatter.13.cloned.1.call-start = ((), (), s32[]{:S(2)}) async-start(), calls=%async_computation.11 | async-start | bytes 442368 | tf_op jit(solution)/shard_map/reduce_scatter | solution.py:220
  545.3 6.8 copy-start.53
  545.4 215.2 %reduce-scatter.15.cloned.1.call-start = ((), (), s32[]{:S(2)}) async-start(), calls=%async_computation.12 | async-start | bytes 442368 | tf_op jit(solution)/shard_map/reduce_scatter | solution.py:170
  547.3 6.3 copy-start.52
  554.2 10.6 %copy-start.24 = (bf16[256,3,2,128]{3,1,0,2:T(4,128)(2,1)S(1)}, bf16[256,3,2,128]{3,1,0,2:T(4,128)(2,1)}, u32[]{:S(2)}) copy-start(bf16[256,3,2,128]{3,1,0,2:T(4,128)(2,1)} %fusion.24) | copy-start | bytes 1179652
  557.0 8.9 %copy-start.46 = (bf16[1,768,256]{2,1,0:T(8,128)(2,1)S(1)}, bf16[1,768,256]{2,1,0:T(8,128)(2,1)}, u32[]{:S(2)}) copy-start(bf16[1,768,256]{2,1,0:T(8,128)(2,1)} %stack_reshape.57) | copy-start | bytes 1179652
  558.0 61.1 %collective-permute-start.5 = (bf16[256,384]{1,0:T(8,128)(2,1)}, bf16[256,384]{1,0:T(8,128)(2,1)}, u32[]{:S(2)}, u32[]{:S(2)}) collective-permute-start(bf16[256,384]{1,0:T(8,128)(2,1)} %copy.313), channel_id=1, source_target_pairs={{0,8},{8,0},{16,24},{24,16},{32,40},{40,32},{48,56},{56,48},{64,72... | collective-permute-start | bytes 589832 | tf_op jit(solution)/shard_map/ppermute | solution.py:17
  565.8 4.1 copy-start.15
  565.8 233.3 %reduce-scatter.11.cloned.1.call-start = ((), (), s32[]{:S(2)}) async-start(), calls=%async_computation.10 | async-start | bytes 2654208 | tf_op jit(solution)/shard_map/reduce_scatter | solution.py:167
  571.6 262.5 %reduce-scatter.17.cloned.1.call-start = ((), (), s32[]{:S(2)}) async-start(), calls=%async_computation.13 | async-start | bytes 221184 | tf_op jit(solution)/shard_map/reduce_scatter | solution.py:173
  573.1 7.3 copy-start.12
  574.2 46.3 %collective-permute-start.6 = (bf16[256,384]{1,0:T(8,128)(2,1)}, bf16[256,384]{1,0:T(8,128)(2,1)S(1)}, u32[]{:S(2)}, u32[]{:S(2)}) collective-permute-start(bf16[256,384]{1,0:T(8,128)(2,1)} %copy.320), channel_id=1, source_target_pairs={{0,16},{16,0},{8,24},{24,8},{32,48},{48,32},{40,56},{56,40},{64,80... | collective-permute-start | bytes 589832 | tf_op jit(solution)/shard_map/ppermute | solution.py:17
  577.0 6.3 copy-start.11
  578.0 44.4 %collective-permute-start.7 = (bf16[256,384]{1,0:T(8,128)(2,1)}, bf16[256,384]{1,0:T(8,128)(2,1)}, u32[]{:S(2)}, u32[]{:S(2)}) collective-permute-start(bf16[256,384]{1,0:T(8,128)(2,1)} %copy.326), channel_id=1, source_target_pairs={{0,32},{32,0},{8,40},{40,8},{16,48},{48,16},{24,56},{56,24},{64,96... | collective-permute-start | bytes 589832 | tf_op jit(solution)/shard_map/ppermute | solution.py:17
  582.6 42.6 %collective-permute-start.8 = (bf16[256,384]{1,0:T(8,128)(2,1)S(1)}, bf16[256,384]{1,0:T(8,128)(2,1)S(1)}, u32[]{:S(2)}, u32[]{:S(2)}) collective-permute-start(bf16[256,384]{1,0:T(8,128)(2,1)S(1)} %copy.332), channel_id=1, source_target_pairs={{0,64},{64,0},{8,72},{72,8},{16,80},{80,16},{24,88},{88,24},{32,96... | collective-permute-start | bytes 589832 | tf_op jit(solution)/shard_map/ppermute | solution.py:17
  586.1 4.6 copy-start.9
  586.1 40.2 %collective-permute-start.9 = (bf16[256,384]{1,0:T(8,128)(2,1)}, bf16[256,384]{1,0:T(8,128)(2,1)S(1)}, u32[]{:S(2)}, u32[]{:S(2)}) collective-permute-start(bf16[256,384]{1,0:T(8,128)(2,1)} %copy.338), channel_id=1, source_target_pairs={{0,128},{128,0},{8,136},{136,8},{16,144},{144,16},{24,152},{152,24... | collective-permute-start | bytes 589832 | tf_op jit(solution)/shard_map/ppermute | solution.py:17
  592.5 3.8 copy-start.5
  595.2 3.8 copy-start.3
  603.7 14.4 %copy-start.45 = (bf16[256,384]{1,0:T(8,128)(2,1)S(1)}, bf16[256,384]{1,0:T(8,128)(2,1)}, u32[]{:S(2)}) copy-start(bf16[256,384]{1,0:T(8,128)(2,1)} %param.10) | copy-start | bytes 589828
  615.3 13.1 %copy-start.54 = (f32[256,384]{1,0:T(8,128)S(1)}, f32[256,384]{1,0:T(8,128)}, u32[]{:S(2)}) copy-start(f32[256,384]{1,0:T(8,128)} %copy.314) | copy-start | bytes 1179652
  615.3 13.1 %copy-start.55 = (bf16[384,256]{1,0:T(8,128)(2,1)S(1)}, bf16[384,256]{1,0:T(8,128)(2,1)}, u32[]{:S(2)}) copy-start(bf16[384,256]{1,0:T(8,128)(2,1)} %param.14) | copy-start | bytes 589828
  615.3 13.1 %copy-start.58 = (bf16[256,256]{1,0:T(8,128)(2,1)S(1)}, bf16[256,256]{1,0:T(8,128)(2,1)}, u32[]{:S(2)}) copy-start(bf16[256,256]{1,0:T(8,128)(2,1)} %all-reduce.4.cloned.1.call-done) | copy-start | bytes 393220
  618.1 38.6 %copy-start.56 = (bf16[256,384]{1,0:T(8,128)(2,1)S(1)}, bf16[256,384]{1,0:T(8,128)(2,1)}, u32[]{:S(2)}) copy-start(bf16[256,384]{1,0:T(8,128)(2,1)} %param.17) | copy-start | bytes 589828
  618.2 216.0 %copy-start.1 = (bf16[256,768]{1,0:T(8,128)(2,1)S(1)}, bf16[256,768]{1,0:T(8,128)(2,1)}, u32[]{:S(2)}) copy-start(bf16[256,768]{1,0:T(8,128)(2,1)} %param.15) | copy-start | bytes 1179652
  619.2 37.5 %collective-permute-start = (bf16[256,384]{1,0:T(8,128)(2,1)}, bf16[256,384]{1,0:T(8,128)(2,1)S(1)}, u32[]{:S(2)}, u32[]{:S(2)}) collective-permute-start(bf16[256,384]{1,0:T(8,128)(2,1)} %copy.251), channel_id=1, source_target_pairs={{0,8},{8,0},{16,24},{24,16},{32,40},{40,32},{48,56},{56,48},{64,72... | collective-permute-start | bytes 589832 | tf_op jit(solution)/shard_map/ppermute | solution.py:17
  620.5 36.2 %collective-permute-start.1 = (bf16[256,384]{1,0:T(8,128)(2,1)}, bf16[256,384]{1,0:T(8,128)(2,1)S(1)}, u32[]{:S(2)}, u32[]{:S(2)}) collective-permute-start(bf16[256,384]{1,0:T(8,128)(2,1)} %copy.258), channel_id=1, source_target_pairs={{0,16},{16,0},{8,24},{24,8},{32,48},{48,32},{40,56},{56,40},{64,80... | collective-permute-start | bytes 589832 | tf_op jit(solution)/shard_map/ppermute | solution.py:17
  622.4 34.3 %collective-permute-start.2 = (bf16[256,384]{1,0:T(8,128)(2,1)}, bf16[256,384]{1,0:T(8,128)(2,1)S(1)}, u32[]{:S(2)}, u32[]{:S(2)}) collective-permute-start(bf16[256,384]{1,0:T(8,128)(2,1)} %copy.264), channel_id=1, source_target_pairs={{0,32},{32,0},{8,40},{40,8},{16,48},{48,16},{24,56},{56,24},{64,96... | collective-permute-start | bytes 589832 | tf_op jit(solution)/shard_map/ppermute | solution.py:17
  625.2 31.5 %collective-permute-start.3 = (bf16[256,384]{1,0:T(8,128)(2,1)}, bf16[256,384]{1,0:T(8,128)(2,1)S(1)}, u32[]{:S(2)}, u32[]{:S(2)}) collective-permute-start(bf16[256,384]{1,0:T(8,128)(2,1)} %copy.270), channel_id=1, source_target_pairs={{0,64},{64,0},{8,72},{72,8},{16,80},{80,16},{24,88},{88,24},{32,96... | collective-permute-start | bytes 589832 | tf_op jit(solution)/shard_map/ppermute | solution.py:17
  626.3 30.4 %collective-permute-start.4 = (bf16[256,384]{1,0:T(8,128)(2,1)}, bf16[256,384]{1,0:T(8,128)(2,1)}, u32[]{:S(2)}, u32[]{:S(2)}) collective-permute-start(bf16[256,384]{1,0:T(8,128)(2,1)} %copy.276), channel_id=1, source_target_pairs={{0,128},{128,0},{8,136},{136,8},{16,144},{144,16},{24,152},{152,24... | collective-permute-start | bytes 589832 | tf_op jit(solution)/shard_map/ppermute | solution.py:17
  (19 other events, 35.9 us)
Sparse Core Ops, SparseCore 0:
  12.1 145.9 all-reduce.5
  161.2 85.5 all-gather.4
  250.0 85.6 all-gather.6
  390.3 138.9 all-reduce.3
  532.0 83.1 all-gather.8
  617.8 37.0 reduce-scatter.8
  658.2 31.7 reduce-scatter.18
  693.0 32.0 reduce-scatter.12
  728.4 32.1 reduce-scatter.14
  763.6 35.5 reduce-scatter.10
  802.3 31.8 reduce-scatter.16
